TPU v7x, 32 devices: a whole 2x2x4 slice. The times are simulated.
32 devices in a mesh: seq: 8 (over z, x), exp: 4 (over y, core).
Axes of the slice: x: 2, y: 2, z: 4, core: 2. Of those that a mesh axis runs over, the one named last changes fastest.
Arguments:
- projected: bfloat16 [4, 1024, 3, 4096], P('exp', 'seq'), may hold values from -8 to 8
- patches: bfloat16 [4, 1024, 4096], P('exp', 'seq'), may hold values from -6 to 6
- norm_gain: float32 [4096], replicated, may hold values from 0.1 to 1.9
- expert_ids: int32 [4, 1024, 2], P('exp', 'seq'), may hold values from 0 to 31, all different within a row; in each aligned block of 128 rows (0 to 127, 128 to 255, ..., all dimensions but the last counted through in order) at most 16 rows name the same one
- gate_levels: int32 [4, 1024, 2], P('exp', 'seq'), may hold values from 1 to 256
- w_gate: bfloat16 [32, 4096, 768], P(('seq', 'exp')), may hold values from -0.09375 to 0.09375
- w_up: bfloat16 [32, 4096, 768], P(('seq', 'exp')), may hold values from -0.09375 to 0.09375
- w_down: bfloat16 [32, 768, 4096], P(('seq', 'exp')), may hold values from -0.21875 to 0.21875
Outputs:
- attended: bfloat16 [4, 1024, 4096], P('exp', 'seq')
- layer_out: bfloat16 [4, 1024, 4096], P('exp', 'seq')
Inputs may be any that keep to these rules, and one draw needn't show every extreme that they name: `expert_ids`: each patch names two different experts. Among the 128 patches of one device (aligned blocks of rows, sequences first), at most 16 name the same expert, and in every draw some expert is named by exactly 16 patches of some device.
All inputs are finite; a program needn't handle non-finite values.
Results may differ from a plain program's by a relative error of at most 0.0068.
Values may be sent and summed in bfloat16 or wider, within the bound.
No kernel may reach another device: no remote copies, remote signals or barrier semaphores. Data moves between devices by JAX's collectives and lax.ppermute only.
A program may use at most 128 MiB of HBM per device.

v0:
```python
import math
import jax
import jax.numpy as jnp
from jax import lax
from jax.sharding import PartitionSpec as P

HEADS = 32


def expert_ffn(arrived, w_gate, w_up, w_down):
    flat_rows = arrived.reshape(-1, arrived.shape[-1])
    gate_part = jnp.dot(flat_rows, w_gate[0], preferred_element_type=jnp.float32)
    up_part = jnp.dot(flat_rows, w_up[0], preferred_element_type=jnp.float32)
    hidden = (jax.nn.silu(gate_part) * up_part).astype(jnp.bfloat16)
    result = jnp.dot(hidden, w_down[0], preferred_element_type=jnp.float32).astype(jnp.bfloat16)
    return result.reshape(arrived.shape[:-1] + (w_down.shape[2],))


def shards(projected, patches, norm_gain, expert_ids, gate_levels, w_gate, w_up, w_down):
    seq_count = lax.axis_size("seq")
    exp_count = lax.axis_size("exp")
    tok_rows = patches.shape[1]
    width = patches.shape[2]
    regrouped = lax.all_to_all(projected, "seq", split_axis=3, concat_axis=1, tiled=True)
    length = regrouped.shape[1]
    local_width = regrouped.shape[3]
    local_heads = HEADS // seq_count
    head_width = local_width // local_heads
    scale = 1.0 / math.sqrt(head_width)
    query_rows = regrouped[0, :, 0].reshape(length, local_heads, head_width)
    key_rows = regrouped[0, :, 1].reshape(length, local_heads, head_width)
    value_rows = regrouped[0, :, 2].reshape(length, local_heads, head_width)
    step_rows = min(512, length)

    def attend(block_index):
        start = block_index * step_rows
        query_part = lax.dynamic_slice_in_dim(query_rows, start, step_rows, 0)
        scores = (
            jnp.einsum("qhd,khd->hqk", query_part, key_rows, preferred_element_type=jnp.float32)
            * scale
        )
        query_pos = start + lax.broadcasted_iota(jnp.int32, (step_rows, length), 0)
        key_pos = lax.broadcasted_iota(jnp.int32, (step_rows, length), 1)
        scores = jnp.where((key_pos <= query_pos)[None], scores, jnp.float32(-1e30))
        highest = jnp.max(scores, axis=-1, keepdims=True)
        weights = jnp.exp(scores - highest)
        probs = (weights / jnp.sum(weights, axis=-1, keepdims=True)).astype(jnp.bfloat16)
        mixed_part = jnp.einsum(
            "hqk,khd->qhd", probs, value_rows, preferred_element_type=jnp.float32
        )
        return mixed_part.astype(jnp.bfloat16).reshape(step_rows, local_width)

    outputs = lax.map(attend, jnp.arange(length // step_rows, dtype=jnp.int32))
    head_major = outputs.reshape(1, length, local_width)
    attended = lax.all_to_all(head_major, "seq", split_axis=1, concat_axis=2, tiled=True)
    stream = (patches.astype(jnp.float32) + attended.astype(jnp.float32)).astype(jnp.bfloat16)
    stream_f = stream.astype(jnp.float32)
    mean_square = jnp.mean(stream_f * stream_f, axis=-1, keepdims=True)
    normed = (stream_f * lax.rsqrt(mean_square + 1e-05) * norm_gain).astype(jnp.bfloat16)
    normed_rows = normed[0]
    expert_count = seq_count * exp_count * w_gate.shape[0]
    capacity = max(2, 4 * tok_rows // expert_count)
    routed = expert_ids[0].reshape(-1)
    onehot = (routed[:, None] == jnp.arange(expert_count, dtype=jnp.int32)[None, :]).astype(
        jnp.int32
    )
    slot = jnp.sum(jnp.cumsum(onehot, axis=0) * onehot, axis=1) - 1
    position = routed * capacity + slot
    selection = jnp.arange(expert_count * capacity, dtype=jnp.int32)[:, None] == position[None, :]
    dispatch_matrix = jnp.any(
        selection.reshape(expert_count * capacity, tok_rows, 2), axis=2
    ).astype(jnp.bfloat16)
    buffer = jnp.dot(dispatch_matrix, normed_rows, preferred_element_type=jnp.float32).astype(
        jnp.bfloat16
    )
    outgoing = buffer.reshape(expert_count, capacity, width)
    processed = expert_ffn(
        lax.all_to_all(outgoing, ("seq", "exp"), split_axis=0, concat_axis=0, tiled=True),
        w_gate,
        w_up,
        w_down,
    )
    returned = lax.all_to_all(processed, ("seq", "exp"), split_axis=0, concat_axis=0, tiled=True)
    flat_back = returned.reshape(expert_count * capacity, width)
    picked = flat_back[position].reshape(tok_rows, 2, width).astype(jnp.float32)
    levels = gate_levels[0].astype(jnp.float32)
    share = levels / jnp.sum(levels, axis=-1, keepdims=True)
    mixture = picked[:, 0, :] * share[:, 0:1] + picked[:, 1, :] * share[:, 1:2]
    layer_out = (stream_f[0] + mixture).astype(jnp.bfloat16)
    return (attended, layer_out[None])


def solution(mesh):
    return jax.shard_map(
        shards,
        mesh=mesh,
        in_specs=(
            P("exp", "seq", None, None),
            P("exp", "seq", None),
            P(),
            P("exp", "seq", None),
            P("exp", "seq", None),
            P(("seq", "exp"), None, None),
            P(("seq", "exp"), None, None),
            P(("seq", "exp"), None, None),
        ),
        out_specs=(P("exp", "seq", None), P("exp", "seq", None)),
        check_vma=False,
    )
```

profile of v0, /device:TPU:0, one launch (start us, length us, event | category | flops | bytes accessed | tf_op | source)
XLA Modules:
  0.0 452.3 jit_solution(14695792651133212737)
XLA Ops:
  0.6 7.2 %copy.54 = bf16[1,128,3,4096]{1,2,0,3:T(4,128)(2,1)} copy(bf16[1,128,3,4096]{3,1,2,0:T(8,128)(2,1)} %param.10) | data formatting | bytes 6291456 | tf_op args[0]
  7.8 7.3 %all-to-all-start = ((bf16[1,128,3,4096]{1,2,0,3:T(4,128)(2,1)}), bf16[1,128,3,4096]{1,2,0,3:T(4,128)(2,1)}, u32[]{:S(2)}, u32[]{:S(2)}) async-start(bf16[1,128,3,4096]{1,2,0,3:T(4,128)(2,1)} %copy.54), calls=%async_computation | async-start | bytes 8388608 | tf_op jit(solution)/shard_map/all_to_all | solution.py:24
  15.1 93.3 %all-to-all-done = bf16[1,128,3,4096]{1,2,0,3:T(4,128)(2,1)} async-done(((bf16[1,128,3,4096]{1,2,0,3:T(4,128)(2,1)}), bf16[1,128,3,4096]{1,2,0,3:T(4,128)(2,1)}, u32[]{:S(2)}, u32[]{:S(2)}) %all-to-all-start) | async-done | bytes 3145760 | tf_op jit(solution)/shard_map/all_to_all | solution.py:24
  108.4 4.8 %copy.81 = bf16[1,128,3,8,512]{1,3,4,2,0:T(8,128)(2,1)S(1)} copy(bf16[1,128,3,8,512]{1,2,4,3,0:T(4,128)(2,1)} %bitcast.3) | data formatting | bytes 6291456 | tf_op jit(solution)/shard_map/all_to_all | solution.py:24
  113.1 3.4 all_to_all.35
  116.5 3.8 fusion.55
  120.9 29.8 %while.10 = (s32[]{:T(128)}, bf16[2,512,512]{2,1,0:T(8,128)(2,1)S(1)}, s32[2]{0:T(128)S(1)}, bf16[1024,4,128]{0,2,1:T(8,128)(2,1)}, bf16[1024,4,128]{2,0,1:T(8,1...) while((s32[]{:T(128)}, ...), condition=%wide.region_3.4_spmd, body=%wide.region_0.3_spmd.sunk | while | flops 1087112704 | bytes 23089332 | solution.py:53
  122.6 7.5 %fusion.70 = (f32[4,512]{1,0:T(4,128)S(1)}, f32[4,512,1024]{2,1,0:T(8,128)}) fusion(pred[512,1024]{1,0:T(8,128)(4,1)S(1)} %iota_compare_fusion.5, bf16[1024,4,128]{2,0,1:T(8,128)(2,1)S(1)} %get-tuple-element.153, bf16[1024,4,128]{0,2,1:T(8,128)(2,1)} %get-tuple-element.152, s32[]{:T(128)S(6)} %select_n.32), kind=kOutput, calls=%fused_computation.67.clone.1 | convolution fusion | flops 545260544 | bytes 10493956 | tf_op jit(solution)/shard_map/while/body/eval_jaxpr/sub | solution.py:46
  130.1 5.2 %fusion.71 = bf16[4,512,128]{1,2,0:T(8,128)(2,1)S(1)} fusion(bf16[1024,4,128]{0,2,1:T(8,128)(2,1)} %get-tuple-element.154, f32[4,512,1024]{2,1,0:T(8,128)} %get-tuple-element.127, f32[4,512]{1,0:T(4,128)S(1)} %get-tuple-element.128), kind=kOutput, calls=%fused_computation.11.clone.1 | convolution fusion | flops 541327360 | bytes 9969664 | tf_op jit(solution)/shard_map/while/body/eval_jaxpr/hqk,khd->qhd/dot_general | solution.py:48
  137.2 7.5 %fusion.70 = (f32[4,512]{1,0:T(4,128)S(1)}, f32[4,512,1024]{2,1,0:T(8,128)}) fusion(pred[512,1024]{1,0:T(8,128)(4,1)S(1)} %iota_compare_fusion.5, bf16[1024,4,128]{2,0,1:T(8,128)(2,1)S(1)} %get-tuple-element.153, bf16[1024,4,128]{0,2,1:T(8,128)(2,1)} %get-tuple-element.152, s32[]{:T(128)S(6)} %select_n.32), kind=kOutput, calls=%fused_computation.67.clone.1 | convolution fusion | flops 545260544 | bytes 10493956 | tf_op jit(solution)/shard_map/while/body/eval_jaxpr/sub | solution.py:46
  144.8 5.2 %fusion.71 = bf16[4,512,128]{1,2,0:T(8,128)(2,1)S(1)} fusion(bf16[1024,4,128]{0,2,1:T(8,128)(2,1)} %get-tuple-element.154, f32[4,512,1024]{2,1,0:T(8,128)} %get-tuple-element.127, f32[4,512]{1,0:T(4,128)S(1)} %get-tuple-element.128), kind=kOutput, calls=%fused_computation.11.clone.1 | convolution fusion | flops 541327360 | bytes 9969664 | tf_op jit(solution)/shard_map/while/body/eval_jaxpr/hqk,khd->qhd/dot_general | solution.py:48
  152.9 7.1 %reduce.4 = bf16[1024,512]{1,0:T(8,128)(2,1)S(1)} reduce(bf16[1024,1,512]{2,1,0:T(2,128)(2,1)S(1)} %bitcast.102, bf16[]{:T(256)} %broadcast.146), dimensions={1}, to_apply=%bitcast.88.reduce_sub_computation | reduce | bytes 2097154
  161.5 3.6 all-to-all-start.1
  168.1 23.0 %all-to-all-done.1 = bf16[8,2,32768]{2,1,0:T(2,128)(2,1)S(1)} async-done(((bf16[8,2,32768]{2,1,0:T(2,128)(2,1)}), bf16[8,2,32768]{2,1,0:T(2,128)(2,1)S(1)}, u32[]{:S(2)}, u32[]{:S(2)}) %all-to-all-start.1) | async-done | bytes 1048608 | tf_op jit(solution)/shard_map/all_to_all | solution.py:55
  196.7 97.1 %all_to_all.46 = bf16[32,16,4096]{2,1,0:T(8,128)(2,1)S(1)} all-to-all(bf16[32,16,4096]{2,1,0:T(8,128)(2,1)S(1)} %bitcast.97), channel_id=1, replica_groups=mesh['seq'=8,'exp'=4] {'seq','exp'}, dimensions={0} | all-to-all | bytes 8388608 | tf_op jit(solution)/shard_map/all_to_all | solution.py:78
  295.8 4.6 %fusion.26 = f32[512,768]{1,0:T(8,128)} fusion(bf16[512,4096]{1,0:T(8,128)(2,1)S(1)} %bitcast.105, bf16[1,4096,768]{2,1,0:T(8,128)(2,1)S(1)} %bitcast.114), kind=kOutput, calls=%fused_computation.26 | convolution fusion | flops 3221225472 | bytes 12058624 | tf_op jit(solution)/shard_map/dot_general | solution.py:12
  300.4 17.0 %fusion.28 = bf16[512,4096]{1,0:T(8,128)(2,1)} fusion(bf16[1,768,4096]{2,1,0:T(8,128)(2,1)} %param.17, f32[512,768]{1,0:T(8,128)} %fusion.26, bf16[512,4096]{1,0:T(8,128)(2,1)} %bitcast.106, bf16[1,4096,768]{2,1,0:T(8,128)(2,1)} %param.16), kind=kOutput, calls=%fused_computation.29 | convolution fusion | flops 6446907392 | bytes 22544384 | tf_op jit(solution)/shard_map/dot_general | solution.py:15
  317.4 4.0 all-to-all-start.3
  323.0 92.7 %all-to-all-done.3 = bf16[32,16,4096]{2,1,0:T(8,128)(2,1)} async-done(((bf16[32,16,4096]{2,1,0:T(8,128)(2,1)}), bf16[32,16,4096]{2,1,0:T(8,128)(2,1)}, u32[]{:S(2)}, u32[]{:S(2)}) %all-to-all-start.3) | async-done | bytes 4194336 | tf_op jit(solution)/shard_map/all_to_all | solution.py:83
  415.7 6.6 %gather_fusion = bf16[256,4096]{1,0:T(8,128)(2,1)S(1)} fusion(bf16[512,4096]{1,0:T(8,128)(2,1)} %bitcast.20, s32[1024]{0:T(1024)S(1)} %pad_clamp_fusion), kind=kCustom, calls=%fused_computation | custom fusion | bytes 4195328 | tf_op jit(solution)/shard_map/gather | solution.py:85
  422.3 4.0 reshape.229
  426.3 9.9 %fusion.54 = (f32[128,1,4096]{2,1,0:T(1,128)}, f32[128,1,4096]{2,1,0:T(1,128)}) fusion(f32[128,2,4096]{2,1,0:T(2,128)} %reshape.229), kind=kLoop, calls=%fused_computation.68 | loop fusion | bytes 8388608 | tf_op jit(solution)/shard_map/slice | solution.py:88
  436.1 5.0 %copy.76 = f32[128,1,4096]{0,2,1:T(8,128)S(1)} copy(f32[128,1,4096]{2,1,0:T(1,128)} %get-tuple-element.82) | data formatting | bytes 4194304
  441.2 5.6 %copy.75 = f32[128,1,4096]{0,2,1:T(8,128)} copy(f32[128,1,4096]{2,1,0:T(1,128)} %get-tuple-element.81) | data formatting | bytes 4194304
  (64 shorter events, 24.0 us)
Async XLA Ops:
  7.8 100.6 %all-to-all-start = ((bf16[1,128,3,4096]{1,2,0,3:T(4,128)(2,1)}), bf16[1,128,3,4096]{1,2,0,3:T(4,128)(2,1)}, u32[]{:S(2)}, u32[]{:S(2)}) async-start(bf16[1,128,3,4096]{1,2,0,3:T(4,128)(2,1)} %copy.54), calls=%async_computation | async-start | bytes 8388608 | tf_op jit(solution)/shard_map/all_to_all | solution.py:24
  116.5 4.4 copy-start.1
  152.9 12.3 %copy-start.4 = (s32[1,128,2]{1,2,0:T(2,128)S(1)}, s32[1,128,2]{1,2,0:T(2,128)}, u32[]{:S(2)}) copy-start(s32[1,128,2]{1,2,0:T(2,128)} %param.13) | copy-start | bytes 3076
  159.9 5.6 %copy-start.2 = (bf16[1,128,4096]{2,1,0:T(8,128)(2,1)S(1)}, bf16[1,128,4096]{2,1,0:T(8,128)(2,1)}, u32[]{:S(2)}) copy-start(bf16[1,128,4096]{2,1,0:T(8,128)(2,1)} %param.11) | copy-start | bytes 3145732
  161.5 29.6 %all-to-all-start.1 = ((bf16[8,2,32768]{2,1,0:T(2,128)(2,1)}), bf16[8,2,32768]{2,1,0:T(2,128)(2,1)S(1)}, u32[]{:S(2)}, u32[]{:S(2)}) async-start(bf16[8,2,32768]{2,1,0:T(2,128)(2,1)} %reshape.239), calls=%async_computation.1 | async-start | bytes 2097152 | tf_op jit(solution)/shard_map/all_to_all | solution.py:55
  192.4 2.5 copy-start.3
  195.0 100.8 %slice-start = ((s8[6291456]{0:T(1024)(128)(4,1)}), s8[4194304]{0:T(1024)(128)(4,1)S(1)}, s32[]{:S(2)}) async-start(s8[6291456]{0:T(1024)(128)(4,1)} %bitcast.113), calls=%async_computation.4 | async-start | bytes 8388608
  196.7 99.1 %slice-start.1 = ((s8[6291456]{0:T(1024)(128)(4,1)}), s8[2097152]{0:T(1024)(128)(4,1)S(1)}, s32[]{:S(2)}) async-start(s8[6291456]{0:T(1024)(128)(4,1)} %bitcast.113), calls=%async_computation.5 | async-start | bytes 4194304
  293.8 2.0 copy-start
  317.4 4.2 copy-start.5
  317.4 98.2 %all-to-all-start.3 = ((bf16[32,16,4096]{2,1,0:T(8,128)(2,1)}), bf16[32,16,4096]{2,1,0:T(8,128)(2,1)}, u32[]{:S(2)}, u32[]{:S(2)}) async-start(bf16[32,16,4096]{2,1,0:T(8,128)(2,1)} %bitcast.104), calls=%async_computation.3 | async-start | bytes 8388608 | tf_op jit(solution)/shard_map/all_to_all | solution.py:83
where the time goes:
time: 460 us; the launch traced here: 452 us
  waiting for transfers between devices  209 us (45%)
  blocking collectives  97.1 us (21%)
  local copies, waits for them, and re-layouts  66 us (14%)
  matrix products  48.8 us (11%)
  starting transfers between devices  14.9 us (3%)
  other arithmetic  13.5 us (3%)
    all_to_all x1, blocking collectives, shards(): lax.all_to_all(outgoing, ('seq', 'exp'), split_axis=0, concat_axis=0, til...  97.1 us
    all_to_all x1, waiting for transfers between devices, shards(): lax.all_to_all(projected, 'seq', split_axis=3, concat_axis=1, tiled=True)  93.3 us
    all_to_all x1, waiting for transfers between devices, shards(): lax.all_to_all(processed, ('seq', 'exp'), split_axis=0, concat_axis=0, ti...  92.7 us
    unnamed x27, local copies, waits for them, and re-layouts  28.3 us
    all_to_all x1, waiting for transfers between devices, shards(): lax.all_to_all(head_major, 'seq', split_axis=1, concat_axis=2, tiled=True)  23 us
    dot_general x1, matrix products, expert_ffn(): jnp.dot(hidden, w_down[0], preferred_element_type=jnp.float32)  17 us
    sub x2, matrix products, attend(): weights = jnp.exp(scores - highest)  15.1 us
    dot_general x2, matrix products, attend(): jnp.einsum('hqk,khd->qhd', probs, value_rows, preferred_element_type=jnp....  10.4 us
  transfers between devices with their start and end apart: 3, of which 3 were waited for; matrix products, arithmetic and copies ran while one was open for 1% of the time, Pallas kernels for 0%

commit v1 on v0

--- a/solution.py
+++ b/solution.py
@@ -52,7 +52,18 @@
 
     outputs = lax.map(attend, jnp.arange(length // step_rows, dtype=jnp.int32))
     head_major = outputs.reshape(1, length, local_width)
-    attended = lax.all_to_all(head_major, "seq", split_axis=1, concat_axis=2, tiled=True)
+    ways, here = (lax.axis_size("seq"), lax.axis_index("seq"))
+    width_2 = head_major.shape[1] // ways
+    shape = list(head_major.shape)
+    shape[1] = width_2
+    height = shape[2]
+    shape[2] = height * ways
+    attended = jnp.zeros(shape, head_major.dtype)
+    for mask in range(ways):
+        part = lax.dynamic_slice_in_dim(head_major, (here ^ mask) * width_2, width_2, axis=1)
+        if mask:
+            part = lax.ppermute(part, "seq", [(d, d ^ mask) for d in range(ways)])
+        attended = lax.dynamic_update_slice_in_dim(attended, part, (here ^ mask) * height, axis=2)
     stream = (patches.astype(jnp.float32) + attended.astype(jnp.float32)).astype(jnp.bfloat16)
     stream_f = stream.astype(jnp.float32)
     mean_square = jnp.mean(stream_f * stream_f, axis=-1, keepdims=True)

time: 460 us -> 428 us (0.930); the launches traced: 452 us -> 428 us
  local copies, waits for them, and re-layouts: 66 us -> 46.5 us
  waiting for transfers between devices: 209 us -> 201 us
  starting transfers between devices: 14.9 us -> 22 us
  other arithmetic: 13.5 us -> 7.22 us
    all_to_all x1 -> x0, waiting for transfers between devices: 23 us -> none  [shards(): lax.all_to_all(head_major, 'seq', split_axis=1, concat_axis=2, tiled=True)]
    unnamed x27 -> x24, local copies, waits for them, and re-layouts: 28.3 us -> 9.33 us
    ppermute x0 -> x7, waiting for transfers between devices: none -> 15.3 us  [shards(): part = lax.ppermute(part, 'seq', [(d, d ^ mask) for d in range(ways)])]
    ppermute x0 -> x7, starting transfers between devices: none -> 10.6 us  [shards(): part = lax.ppermute(part, 'seq', [(d, d ^ mask) for d in range(ways)])]
    unnamed x2 -> x1, other arithmetic: 7.06 us -> 0.01 us
  transfers between devices with their start and end apart: 3 -> 9, of which waited for: 3 -> 5; matrix products, arithmetic and copies ran while one was open for 1% -> 0% of each run, Pallas kernels for 0% -> 0%
where the time goes in v1:
time: 428 us
  waiting for transfers between devices  201 us (47%)
  blocking collectives  99.9 us (23%)
  matrix products  48.6 us (11%)
  local copies, waits for them, and re-layouts  46.5 us (11%)
  starting transfers between devices  22 us (5%)
  other arithmetic  7.22 us (2%)
    all_to_all x1, blocking collectives, shards(): lax.all_to_all(outgoing, ('seq', 'exp'), split_axis=0, concat_axis=0, til...  99.9 us
    all_to_all x1, waiting for transfers between devices, shards(): lax.all_to_all(processed, ('seq', 'exp'), split_axis=0, concat_axis=0, ti...  93.8 us
    all_to_all x1, waiting for transfers between devices, shards(): lax.all_to_all(projected, 'seq', split_axis=3, concat_axis=1, tiled=True)  91.7 us
    dot_general x1, matrix products, expert_ffn(): jnp.dot(hidden, w_down[0], preferred_element_type=jnp.float32)  17 us
    ppermute x7, waiting for transfers between devices, shards(): part = lax.ppermute(part, 'seq', [(d, d ^ mask) for d in range(ways)])  15.3 us
    sub x2, matrix products, attend(): weights = jnp.exp(scores - highest)  15.2 us
    ppermute x7, starting transfers between devices, shards(): part = lax.ppermute(part, 'seq', [(d, d ^ mask) for d in range(ways)])  10.6 us
    dot_general x2, matrix products, attend(): jnp.einsum('hqk,khd->qhd', probs, value_rows, preferred_element_type=jnp....  10.4 us
  transfers between devices with their start and end apart: 9, of which 5 were waited for; matrix products, arithmetic and copies ran while one was open for 0% of the time, Pallas kernels for 0%

profile of v1, /device:TPU:0, one launch (start us, length us, event | category | flops | bytes accessed | tf_op | source)
XLA Modules:
  0.0 427.8 jit_solution(7855601794367231271)
XLA Ops:
  0.6 7.2 %copy.36 = bf16[1,128,3,4096]{1,2,0,3:T(4,128)(2,1)} copy(bf16[1,128,3,4096]{3,1,2,0:T(8,128)(2,1)} %param.10) | data formatting | bytes 6291456 | tf_op args[0]
  7.8 7.4 %all-to-all-start = ((bf16[1,128,3,4096]{1,2,0,3:T(4,128)(2,1)}), bf16[1,128,3,4096]{1,2,0,3:T(4,128)(2,1)}, u32[]{:S(2)}, u32[]{:S(2)}) async-start(bf16[1,128,3,4096]{1,2,0,3:T(4,128)(2,1)} %copy.36), calls=%async_computation | async-start | bytes 8388608 | tf_op jit(solution)/shard_map/all_to_all | solution.py:24
  16.8 91.7 %all-to-all-done = bf16[1,128,3,4096]{1,2,0,3:T(4,128)(2,1)} async-done(((bf16[1,128,3,4096]{1,2,0,3:T(4,128)(2,1)}), bf16[1,128,3,4096]{1,2,0,3:T(4,128)(2,1)}, u32[]{:S(2)}, u32[]{:S(2)}) %all-to-all-start) | async-done | bytes 3145760 | tf_op jit(solution)/shard_map/all_to_all | solution.py:24
  108.5 4.8 %copy.68 = bf16[1,128,3,8,512]{1,3,4,2,0:T(8,128)(2,1)S(1)} copy(bf16[1,128,3,8,512]{1,2,4,3,0:T(4,128)(2,1)} %bitcast.3) | data formatting | bytes 6291456 | tf_op jit(solution)/shard_map/all_to_all | solution.py:24
  113.3 3.3 all_to_all.22
  116.6 3.7 fusion.57
  121.0 29.7 %while.10 = (s32[]{:T(128)}, bf16[2,512,512]{2,1,0:T(8,128)(2,1)S(1)}, s32[2]{0:T(128)S(1)}, bf16[1024,4,128]{0,2,1:T(8,128)(2,1)}, bf16[1024,4,128]{2,0,1:T(8,1...) while((s32[]{:T(128)}, ...), condition=%wide.region_3.4_spmd, body=%wide.region_0.3_spmd.sunk | while | flops 1087112704 | bytes 23089332 | solution.py:53
  122.6 7.6 %fusion.72 = (f32[4,512]{1,0:T(4,128)S(1)}, f32[4,512,1024]{2,1,0:T(8,128)}) fusion(pred[512,1024]{1,0:T(8,128)(4,1)S(1)} %iota_compare_fusion.5, bf16[1024,4,128]{2,0,1:T(8,128)(2,1)S(1)} %get-tuple-element.147, bf16[1024,4,128]{0,2,1:T(8,128)(2,1)} %get-tuple-element.146, s32[]{:T(128)S(6)} %select_n.96), kind=kOutput, calls=%fused_computation.84.clone.1 | convolution fusion | flops 545260544 | bytes 10493956 | tf_op jit(solution)/shard_map/while/body/eval_jaxpr/sub | solution.py:46
  130.2 5.2 %fusion.73 = bf16[4,512,128]{1,2,0:T(8,128)(2,1)S(1)} fusion(bf16[1024,4,128]{0,2,1:T(8,128)(2,1)} %get-tuple-element.148, f32[4,512,1024]{2,1,0:T(8,128)} %get-tuple-element.121, f32[4,512]{1,0:T(4,128)S(1)} %get-tuple-element.122), kind=kOutput, calls=%fused_computation.11.clone.1 | convolution fusion | flops 541327360 | bytes 9969664 | tf_op jit(solution)/shard_map/while/body/eval_jaxpr/hqk,khd->qhd/dot_general | solution.py:48
  137.4 7.6 %fusion.72 = (f32[4,512]{1,0:T(4,128)S(1)}, f32[4,512,1024]{2,1,0:T(8,128)}) fusion(pred[512,1024]{1,0:T(8,128)(4,1)S(1)} %iota_compare_fusion.5, bf16[1024,4,128]{2,0,1:T(8,128)(2,1)S(1)} %get-tuple-element.147, bf16[1024,4,128]{0,2,1:T(8,128)(2,1)} %get-tuple-element.146, s32[]{:T(128)S(6)} %select_n.96), kind=kOutput, calls=%fused_computation.84.clone.1 | convolution fusion | flops 545260544 | bytes 10493956 | tf_op jit(solution)/shard_map/while/body/eval_jaxpr/sub | solution.py:46
  145.0 5.2 %fusion.73 = bf16[4,512,128]{1,2,0:T(8,128)(2,1)S(1)} fusion(bf16[1024,4,128]{0,2,1:T(8,128)(2,1)} %get-tuple-element.148, f32[4,512,1024]{2,1,0:T(8,128)} %get-tuple-element.121, f32[4,512]{1,0:T(4,128)S(1)} %get-tuple-element.122), kind=kOutput, calls=%fused_computation.11.clone.1 | convolution fusion | flops 541327360 | bytes 9969664 | tf_op jit(solution)/shard_map/while/body/eval_jaxpr/hqk,khd->qhd/dot_general | solution.py:48
  153.3 2.1 collective-permute-start.2
  156.2 3.0 collective-permute-start.4
  164.2 9.8 %collective-permute-done.3 = bf16[1,128,512]{2,1,0:T(8,128)(2,1)S(1)} collective-permute-done((bf16[1,128,512]{2,1,0:T(8,128)(2,1)}, bf16[1,128,512]{2,1,0:T(8,128)(2,1)S(1)}, u32[]{:S(2)}, u32[]{:S(2)}) %collective-permute-start.3) | collective-permute-done | bytes 131104 | tf_op jit(solution)/shard_map/ppermute | solution.py:65
  174.1 3.7 collective-permute-done.4
  179.7 99.9 %all_to_all.28 = bf16[32,16,4096]{2,1,0:T(8,128)(2,1)S(1)} all-to-all(bf16[32,16,4096]{2,1,0:T(8,128)(2,1)S(1)} %bitcast.91), channel_id=1, replica_groups=mesh['seq'=8,'exp'=4] {'seq','exp'}, dimensions={0} | all-to-all | bytes 8388608 | tf_op jit(solution)/shard_map/all_to_all | solution.py:89
  281.6 4.6 %fusion.26 = f32[512,768]{1,0:T(8,128)} fusion(bf16[512,4096]{1,0:T(8,128)(2,1)S(1)} %bitcast.95, bf16[1,4096,768]{2,1,0:T(8,128)(2,1)S(1)} %bitcast.104), kind=kOutput, calls=%fused_computation.26 | convolution fusion | flops 3221225472 | bytes 12058624 | tf_op jit(solution)/shard_map/dot_general | solution.py:12
  286.2 17.0 %fusion.28 = bf16[512,4096]{1,0:T(8,128)(2,1)} fusion(bf16[1,768,4096]{2,1,0:T(8,128)(2,1)} %param.17, f32[512,768]{1,0:T(8,128)} %fusion.26, bf16[512,4096]{1,0:T(8,128)(2,1)} %bitcast.96, bf16[1,4096,768]{2,1,0:T(8,128)(2,1)} %param.16), kind=kOutput, calls=%fused_computation.29 | convolution fusion | flops 6446907392 | bytes 22544384 | tf_op jit(solution)/shard_map/dot_general | solution.py:15
  303.2 4.0 all-to-all-start.2
  307.5 93.8 %all-to-all-done.2 = bf16[32,16,4096]{2,1,0:T(8,128)(2,1)} async-done(((bf16[32,16,4096]{2,1,0:T(8,128)(2,1)}), bf16[32,16,4096]{2,1,0:T(8,128)(2,1)}, u32[]{:S(2)}, u32[]{:S(2)}) %all-to-all-start.2) | async-done | bytes 4194336 | tf_op jit(solution)/shard_map/all_to_all | solution.py:94
  401.3 7.9 %gather_fusion = bf16[256,4096]{1,0:T(8,128)(2,1)} fusion(bf16[512,4096]{1,0:T(8,128)(2,1)} %bitcast.18, s32[1024]{0:T(1024)S(1)} %pad_clamp_fusion), kind=kCustom, calls=%fused_computation | custom fusion | bytes 4195328 | tf_op jit(solution)/shard_map/gather | solution.py:96
  409.2 5.5 %reshape.217 = f32[128,2,4096]{2,1,0:T(2,128)} reshape(bf16[256,4096]{1,0:T(8,128)(2,1)} %gather_fusion) | data formatting | bytes 6291456 | tf_op jit(solution)/shard_map/convert_element_type | solution.py:96
  414.7 7.9 %fusion.56 = (f32[128,1,4096]{2,1,0:T(1,128)S(1)}, f32[128,1,4096]{2,1,0:T(1,128)S(1)}) fusion(f32[128,2,4096]{2,1,0:T(2,128)} %reshape.217), kind=kLoop, calls=%fused_computation.85 | loop fusion | bytes 8388608 | tf_op jit(solution)/shard_map/slice | solution.py:99
  422.6 5.2 %fusion.34 = bf16[1,128,4096]{2,1,0:T(8,128)(2,1)} fusion(f32[128,1,4096]{2,1,0:T(1,128)S(1)} %get-tuple-element.68, f32[128,1,4096]{2,1,0:T(1,128)S(1)} %get-tuple-element.67, f32[128]{0:T(128)S(1)} %get-tuple-element.81, f32[128]{0:T(128)S(1)} %get-tuple-element.80, bf16[1,128,4096]{2,1,0:T(8,128)(2,1)S(1)} %constant_dynamic-update-slice_fusion.1, ...), kind=kLoop, calls=%fused_computation.37 | loop fusion | flops 5242880 | bytes 7341056 | tf_op jit(solution)/shard_map/convert_element_type | solution.py:100
  (79 shorter events, 16.9 us)
Async XLA Ops:
  7.8 7.4 %copy-start.7 = (s32[1,128,2]{1,2,0:T(2,128)S(1)}, s32[1,128,2]{1,2,0:T(2,128)}, u32[]{:S(2)}) copy-start(s32[1,128,2]{1,2,0:T(2,128)} %param.13) | copy-start | bytes 3076
  7.8 100.7 %all-to-all-start = ((bf16[1,128,3,4096]{1,2,0,3:T(4,128)(2,1)}), bf16[1,128,3,4096]{1,2,0,3:T(4,128)(2,1)}, u32[]{:S(2)}, u32[]{:S(2)}) async-start(bf16[1,128,3,4096]{1,2,0,3:T(4,128)(2,1)} %copy.36), calls=%async_computation | async-start | bytes 8388608 | tf_op jit(solution)/shard_map/all_to_all | solution.py:24
  16.6 91.9 %copy-start.5 = (s32[256]{0:T(256)}, s32[256]{0:T(256)S(1)}, u32[]{:S(2)}) copy-start(s32[256]{0:T(256)S(1)} %broadcast_add_fusion) | copy-start | bytes 3076
  116.6 4.3 %copy-start.3 = (bf16[2,512,512]{2,1,0:T(8,128)(2,1)S(1)}, bf16[2,512,512]{2,1,0:T(8,128)(2,1)}, u32[]{:S(2)}) copy-start(bf16[2,512,512]{2,1,0:T(8,128)(2,1)} %custom-call.2) | copy-start | bytes 3145732
  150.7 27.2 %copy-start.1 = (bf16[1,128,4096]{2,1,0:T(8,128)(2,1)S(1)}, bf16[1,128,4096]{2,1,0:T(8,128)(2,1)}, u32[]{:S(2)}) copy-start(bf16[1,128,4096]{2,1,0:T(8,128)(2,1)} %param.11) | copy-start | bytes 3145732
  150.8 27.6 %copy-start.4 = (f32[4096]{0:T(1024)S(1)}, f32[4096]{0:T(1024)}, u32[]{:S(2)}) copy-start(f32[4096]{0:T(1024)} %param.12) | copy-start | bytes 49156
  151.6 7.6 %collective-permute-start = (bf16[1,128,512]{2,1,0:T(8,128)(2,1)}, bf16[1,128,512]{2,1,0:T(8,128)(2,1)S(1)}, u32[]{:S(2)}, u32[]{:S(2)}) collective-permute-start(bf16[1,128,512]{2,1,0:T(8,128)(2,1)} %get-tuple-element.78), channel_id=1, source_target_pairs={{0,4},{4,0},{8,12},{12,8},{16,20},{20,16},{24,28},{28,24},{1,5},{5... | collective-permute-start | bytes 393224 | tf_op jit(solution)/shard_map/ppermute | solution.py:65
  153.2 9.3 %collective-permute-start.1 = (bf16[1,128,512]{2,1,0:T(8,128)(2,1)}, bf16[1,128,512]{2,1,0:T(8,128)(2,1)S(1)}, u32[]{:S(2)}, u32[]{:S(2)}) collective-permute-start(bf16[1,128,512]{2,1,0:T(8,128)(2,1)} %get-tuple-element.77), channel_id=1, source_target_pairs={{0,8},{4,12},{8,0},{12,4},{16,24},{20,28},{24,16},{28,20},{1,9},{5... | collective-permute-start | bytes 393224 | tf_op jit(solution)/shard_map/ppermute | solution.py:65
  153.3 10.9 %collective-permute-start.2 = (bf16[1,128,512]{2,1,0:T(8,128)(2,1)}, bf16[1,128,512]{2,1,0:T(8,128)(2,1)S(1)}, u32[]{:S(2)}, u32[]{:S(2)}) collective-permute-start(bf16[1,128,512]{2,1,0:T(8,128)(2,1)} %get-tuple-element.76), channel_id=1, source_target_pairs={{0,12},{4,8},{8,4},{12,0},{16,28},{20,24},{24,20},{28,16},{1,13},{... | collective-permute-start | bytes 393224 | tf_op jit(solution)/shard_map/ppermute | solution.py:65
  155.4 18.6 %collective-permute-start.3 = (bf16[1,128,512]{2,1,0:T(8,128)(2,1)}, bf16[1,128,512]{2,1,0:T(8,128)(2,1)S(1)}, u32[]{:S(2)}, u32[]{:S(2)}) collective-permute-start(bf16[1,128,512]{2,1,0:T(8,128)(2,1)} %get-tuple-element.75), channel_id=1, source_target_pairs={{0,16},{4,20},{8,24},{12,28},{16,0},{20,4},{24,8},{28,12},{1,17},{... | collective-permute-start | bytes 393224 | tf_op jit(solution)/shard_map/ppermute | solution.py:65
  156.2 21.6 %collective-permute-start.4 = (bf16[1,128,512]{2,1,0:T(8,128)(2,1)}, bf16[1,128,512]{2,1,0:T(8,128)(2,1)S(1)}, u32[]{:S(2)}, u32[]{:S(2)}) collective-permute-start(bf16[1,128,512]{2,1,0:T(8,128)(2,1)} %get-tuple-element.74), channel_id=1, source_target_pairs={{0,20},{4,16},{8,28},{12,24},{16,4},{20,0},{24,12},{28,8},{1,21},{... | collective-permute-start | bytes 393224 | tf_op jit(solution)/shard_map/ppermute | solution.py:65
  159.2 18.6 %collective-permute-start.5 = (bf16[1,128,512]{2,1,0:T(8,128)(2,1)S(1)}, bf16[1,128,512]{2,1,0:T(8,128)(2,1)S(1)}, u32[]{:S(2)}, u32[]{:S(2)}) collective-permute-start(bf16[1,128,512]{2,1,0:T(8,128)(2,1)S(1)} %get-tuple-element.73), channel_id=1, source_target_pairs={{0,24},{4,28},{8,16},{12,20},{16,8},{20,12},{24,0},{28,4},{1,25},{... | collective-permute-start | bytes 393224 | tf_op jit(solution)/shard_map/ppermute | solution.py:65
  162.4 15.4 %collective-permute-start.6 = (bf16[1,128,512]{2,1,0:T(8,128)(2,1)S(1)}, bf16[1,128,512]{2,1,0:T(8,128)(2,1)S(1)}, u32[]{:S(2)}, u32[]{:S(2)}) collective-permute-start(bf16[1,128,512]{2,1,0:T(8,128)(2,1)S(1)} %get-tuple-element.72), channel_id=1, source_target_pairs={{0,28},{4,24},{8,20},{12,16},{16,12},{20,8},{24,4},{28,0},{1,29},{... | collective-permute-start | bytes 393224 | tf_op jit(solution)/shard_map/ppermute | solution.py:65
  174.0 107.5 %slice-start = ((s8[6291456]{0:T(1024)(128)(4,1)}), s8[4194304]{0:T(1024)(128)(4,1)S(1)}, s32[]{:S(2)}) async-start(s8[6291456]{0:T(1024)(128)(4,1)} %bitcast.103), calls=%async_computation.3 | async-start | bytes 8388608
  177.9 244.7 %copy-start = (bf16[1,128,4096]{2,1,0:T(8,128)(2,1)}, bf16[1,128,4096]{2,1,0:T(8,128)(2,1)S(1)}, u32[]{:S(2)}) copy-start(bf16[1,128,4096]{2,1,0:T(8,128)(2,1)S(1)} %constant_dynamic-update-slice_fusion.1) | copy-start | bytes 3145732
  178.4 103.2 %slice-start.1 = ((s8[6291456]{0:T(1024)(128)(4,1)}), s8[2097152]{0:T(1024)(128)(4,1)S(1)}, s32[]{:S(2)}) async-start(s8[6291456]{0:T(1024)(128)(4,1)} %bitcast.103), calls=%async_computation.4 | async-start | bytes 4194304
  279.6 2.0 copy-start.2
  303.2 4.2 copy-start.8
  303.2 4.2 copy-start.6
  303.2 98.1 %all-to-all-start.2 = ((bf16[32,16,4096]{2,1,0:T(8,128)(2,1)}), bf16[32,16,4096]{2,1,0:T(8,128)(2,1)}, u32[]{:S(2)}, u32[]{:S(2)}) async-start(bf16[32,16,4096]{2,1,0:T(8,128)(2,1)} %bitcast.94), calls=%async_computation.2 | async-start | bytes 8388608 | tf_op jit(solution)/shard_map/all_to_all | solution.py:94
